TPU v7x, 32 devices: a whole 2x2x4 slice. The times are simulated.
32 devices in a mesh: dp: 8 (over y, x, core), tp: 4 (over z).
Axes of the slice: x: 2, y: 2, z: 4, core: 2. Of those that a mesh axis runs over, the one named last changes fastest.
Arguments:
- hidden: bfloat16 [32, 512, 1024], P(('dp', 'tp')), may hold values from -6 to 6
- cell_ids: int32 [32, 512], P(('dp', 'tp')), may hold values from 0 to 63, never falling along the last dimension, each value on 1 to 60 neighbouring positions
- cell_boxes: int32 [32, 64, 4], P(('dp', 'tp')), may hold values from 0 to 1000
- cotangent: bfloat16 [32, 512, 1024], P(('dp', 'tp')), may hold values from -6 to 6
- weight_cols: bfloat16 [7, 1024, 1024], P(None, None, 'tp'), may hold values from -0.1875 to 0.1875
- weight_out: bfloat16 [1024, 1024], P('tp'), may hold values from -1.5 to 1.5
- weight_down: bfloat16 [4, 1024, 1024], P(None, 'tp'), may hold values from -0.09375 to 0.09375
- vectors: float32 [1024, 12], replicated
- vector_moment: float32 [1024, 12], P('dp')
- left_stat: float32 [16, 1024, 1024], P('dp', 'tp')
- right_stat: float32 [16, 1024, 1024], P('dp', 'tp')
- left_root: float32 [16, 1024, 1024], P('dp', 'tp')
- right_root: float32 [16, 1024, 1024], P('dp')
- master: float32 [16, 1024, 1024], P('dp', 'tp'), may hold values from -0.1875 to 0.1875
- averaged_weight: float32 [16, 1024, 1024], P('dp', 'tp'), may hold values from -0.1875 to 0.1875
Outputs:
- layer_out: float32 [32, 512, 1024], P(('dp', 'tp'))
- input_grad: float32 [32, 512, 1024], P(('dp', 'tp'))
- block_grad: float32 [16, 1024, 1024], P('dp', None, 'tp')
- left_new: float32 [16, 1024, 1024], P('dp', 'tp')
- right_new: float32 [16, 1024, 1024], P('dp', 'tp')
- master_new: float32 [16, 1024, 1024], P('dp', 'tp')
- weight_copy: bfloat16 [16, 1024, 1024], P('dp', 'tp')
- ema_new: float32 [16, 1024, 1024], P('dp', 'tp')
- vector_grad: float32 [1024, 12], P('dp')
- moment_new: float32 [1024, 12], P('dp')
- vector_new: float32 [1024, 12], P('dp')
- bias_grad: float32 [1024], P('dp')
Inputs may be any that keep to these rules, and one draw needn't show every extreme that they name: `cell_ids`: on each page cell numbers never fall; each cell spans 1 to 60 consecutive tokens and some cell exactly 60.
All inputs are finite; a program needn't handle non-finite values.
Results may differ from a plain program's by a relative error of at most 0.022.
The roundings to bfloat16 on the way count: a program that leaves them out, or rounds other values in their place, can miss the bound.
Values may be sent and summed in bfloat16 or wider, within the bound.
A program may use at most 256 MiB of HBM per device.

v0:
```python
import math

import jax
import jax.numpy as jnp
from jax import lax
from jax.sharding import PartitionSpec as P

MODEL_WIDTH = 1024
H = 16
HD = 64


PRECISE = lax.Precision.HIGHEST
EPS_NORM = 1e-06
STAT_DECAY = 0.5
BLOCK_RATE = 0.7
EMA_DECAY = 0.9
MOMENTUM = 0.9
VEC_RATE = 0.2


def layout_embed(cell_boxes, cell_ids):
    cell_count = cell_boxes.shape[1]
    onehot = (
        cell_ids[:, :, None] == jnp.arange(cell_count, dtype=jnp.int32)[None, None, :]
    ).astype(jnp.float32)
    corners = jnp.einsum("psc,pck->psk", onehot, cell_boxes.astype(jnp.float32), precision=PRECISE)
    quarter = MODEL_WIDTH // 4
    half_width = quarter // 2
    frequency = jnp.exp(
        -jnp.arange(half_width, dtype=jnp.float32) * (math.log(1000.0) / half_width)
    )
    angle_grid = corners[..., None] * frequency
    wave_table = jnp.concatenate([jnp.sin(angle_grid), jnp.cos(angle_grid)], -1)
    return 0.5 * wave_table.reshape(corners.shape[0], corners.shape[1], MODEL_WIDTH)


def gelu_exact(values):
    return jax.nn.gelu(values, approximate=False)


def norm_forward(values, gain, shift):
    center = values - jnp.mean(values, -1, keepdims=True)
    inv_std = lax.rsqrt(jnp.mean(center * center, -1, keepdims=True) + EPS_NORM)
    normed = center * inv_std
    return (normed * gain + shift, normed, inv_std)


def norm_backward(grad_in, normed, inv_std, gain):
    scaled = grad_in * gain
    grad_arg = inv_std * (
        scaled
        - jnp.mean(scaled, -1, keepdims=True)
        - normed * jnp.mean(scaled * normed, -1, keepdims=True)
    )
    return (grad_arg, jnp.sum(grad_in * normed, (0, 1)), jnp.sum(grad_in, (0, 1)))


def attend(query_low, key_low, value_low, head_count):
    groups, seq_len = (query_low.shape[0], query_low.shape[1])
    shape_heads = (groups, seq_len, head_count, HD)
    scores = jnp.einsum(
        "gqhe,gkhe->ghqk",
        query_low.reshape(shape_heads),
        key_low.reshape(shape_heads),
        preferred_element_type=jnp.float32,
    ) * HD ** (-0.5)
    row_max = jnp.max(scores, -1, keepdims=True)
    log_total = row_max + jnp.log(jnp.sum(jnp.exp(scores - row_max), -1, keepdims=True))
    probs = jnp.exp(scores - log_total).astype(jnp.bfloat16)
    context = jnp.einsum(
        "ghqk,gkhe->gqhe", probs, value_low.reshape(shape_heads), preferred_element_type=jnp.float32
    )
    return (context.reshape(groups, seq_len, head_count * HD).astype(jnp.bfloat16), log_total)


def attend_back(query_low, key_low, value_low, log_total, ctx_grad, head_count):
    groups, seq_len = (query_low.shape[0], query_low.shape[1])
    shape_heads = (groups, seq_len, head_count, HD)
    query_heads = query_low.reshape(shape_heads)
    key_heads = key_low.reshape(shape_heads)
    value_heads = value_low.reshape(shape_heads)
    grad_heads = ctx_grad.reshape(shape_heads)
    scale = HD ** (-0.5)
    scores = (
        jnp.einsum("gqhe,gkhe->ghqk", query_heads, key_heads, preferred_element_type=jnp.float32)
        * scale
    )
    probs = jnp.exp(scores - log_total)
    value_grad = jnp.einsum(
        "ghqk,gqhe->gkhe",
        probs.astype(jnp.bfloat16),
        grad_heads,
        preferred_element_type=jnp.float32,
    )
    prob_grad = jnp.einsum(
        "gqhe,gkhe->ghqk", grad_heads, value_heads, preferred_element_type=jnp.float32
    )
    score_grad = (probs * (prob_grad - jnp.sum(probs * prob_grad, -1, keepdims=True))).astype(
        jnp.bfloat16
    )
    query_grad = (
        jnp.einsum("ghqk,gkhe->gqhe", score_grad, key_heads, preferred_element_type=jnp.float32)
        * scale
    )
    key_grad = (
        jnp.einsum("ghqk,gqhe->gkhe", score_grad, query_heads, preferred_element_type=jnp.float32)
        * scale
    )
    width = head_count * HD
    return (
        query_grad.reshape(groups, seq_len, width).astype(jnp.bfloat16),
        key_grad.reshape(groups, seq_len, width).astype(jnp.bfloat16),
        value_grad.reshape(groups, seq_len, width).astype(jnp.bfloat16),
    )


def local(
    hidden,
    cell_ids,
    cell_boxes,
    cotangent,
    weight_cols,
    weight_out,
    weight_down,
    vectors,
    vector_moment,
    left_stat,
    right_stat,
    left_root,
    right_root,
    master,
    averaged_weight,
):
    tp_count = lax.axis_size("tp")
    dp_count = lax.axis_size("dp")
    tp_index = lax.axis_index("tp")
    dp_index = lax.axis_index("dp")
    strip_width = weight_cols.shape[2]
    page_rows, seq_len = (hidden.shape[0], hidden.shape[1])
    x_own = hidden.astype(jnp.float32) + layout_embed(cell_boxes, cell_ids)
    x_low = x_own.astype(jnp.bfloat16)
    col_mats, out_mat, down_mats = (weight_cols, weight_out, weight_down)
    x_input = lax.all_gather(x_low, "tp", axis=0, tiled=True)
    head_count = H // tp_count
    bias_cols = lax.dynamic_slice_in_dim(vectors, tp_index * strip_width, strip_width, 0)[:, 6:]
    projected = jnp.einsum(
        "gtd,kdc->kgtc", x_input, col_mats[0:3], preferred_element_type=jnp.float32
    )
    query_low = (projected[0] + bias_cols[:, 0]).astype(jnp.bfloat16)
    key_low = projected[1].astype(jnp.bfloat16)
    value_low = (projected[2] + bias_cols[:, 1]).astype(jnp.bfloat16)
    context, log_total = attend(query_low, key_low, value_low, head_count)
    attn_out = lax.psum_scatter(
        jnp.einsum("gtc,cd->gtd", context, out_mat, preferred_element_type=jnp.float32).astype(
            jnp.bfloat16
        ),
        "tp",
        scatter_dimension=0,
        tiled=True,
    ).astype(jnp.float32)
    mid_out, mid_hat, mid_inv = norm_forward(
        x_own + attn_out + vectors[:, 0], vectors[:, 2], vectors[:, 3]
    )
    mid_low = mid_out.astype(jnp.bfloat16)
    mid_input = lax.all_gather(mid_low, "tp", axis=0, tiled=True)
    up_pre = jnp.einsum(
        "gtd,kdc->kgtc", mid_input, col_mats[3:7], preferred_element_type=jnp.float32
    )
    up_pre = up_pre + jnp.transpose(bias_cols[:, 2:6])[:, None, None, :]
    act_low = gelu_exact(up_pre).astype(jnp.bfloat16)
    ffn_out = lax.psum_scatter(
        jnp.einsum("kgtc,kcd->gtd", act_low, down_mats, preferred_element_type=jnp.float32).astype(
            jnp.bfloat16
        ),
        "tp",
        scatter_dimension=0,
        tiled=True,
    ).astype(jnp.float32)
    layer_out, out_hat, out_inv = norm_forward(
        mid_out + ffn_out + vectors[:, 1], vectors[:, 4], vectors[:, 5]
    )
    output_gradient = cotangent.astype(jnp.float32)
    grad_two, gain_two, shift_two = norm_backward(output_gradient, out_hat, out_inv, vectors[:, 4])
    two_low = grad_two.astype(jnp.bfloat16)
    two_input = lax.all_gather(two_low, "tp", axis=0, tiled=True)
    act_grad = jnp.einsum("gtd,kcd->kgtc", two_input, down_mats, preferred_element_type=jnp.float32)
    gelu_pull = jax.vjp(gelu_exact, up_pre)[1]
    up_low = gelu_pull(act_grad)[0].astype(jnp.bfloat16)
    mid_back = lax.psum_scatter(
        jnp.einsum(
            "kgtc,kdc->gtd", up_low, col_mats[3:7], preferred_element_type=jnp.float32
        ).astype(jnp.bfloat16),
        "tp",
        scatter_dimension=0,
        tiled=True,
    ).astype(jnp.float32)
    grad_one, gain_one, shift_one = norm_backward(
        mid_back + grad_two, mid_hat, mid_inv, vectors[:, 2]
    )
    one_low = grad_one.astype(jnp.bfloat16)
    one_input = lax.all_gather(one_low, "tp", axis=0, tiled=True)
    ctx_grad = jnp.einsum(
        "gtd,cd->gtc", one_input, out_mat, preferred_element_type=jnp.float32
    ).astype(jnp.bfloat16)
    query_grad, key_grad, value_grad = attend_back(
        query_low, key_low, value_low, log_total, ctx_grad, head_count
    )
    qkv_grad = jnp.stack([query_grad, key_grad, value_grad], 0)
    input_part = jnp.einsum(
        "kgtc,kdc->gtd", qkv_grad, col_mats[0:3], preferred_element_type=jnp.float32
    )
    unit_width = query_low.shape[2]
    strip_parts = unit_width // strip_width

    def split_units(array):
        return array.reshape(array.shape[:-1] + (strip_parts, strip_width))

    qkv_blocks = jnp.einsum(
        "gtd,kgtnc->nkdc", x_input, split_units(qkv_grad), preferred_element_type=jnp.float32
    )
    up_blocks = jnp.einsum(
        "gtd,kgtnc->nkdc", mid_input, split_units(up_low), preferred_element_type=jnp.float32
    )
    out_block = jnp.einsum(
        "gtnc,gtd->ndc", split_units(context), one_input, preferred_element_type=jnp.float32
    )
    down_blocks = jnp.einsum(
        "kgtnc,gtd->nkdc", split_units(act_low), two_input, preferred_element_type=jnp.float32
    )
    all_blocks = jnp.concatenate([qkv_blocks, up_blocks, out_block[:, None], down_blocks], 1)
    shared_part = jnp.stack(
        [
            jnp.sum(grad_one, (0, 1)),
            jnp.sum(grad_two, (0, 1)),
            gain_one,
            shift_one,
            gain_two,
            shift_two,
        ],
        1,
    )
    unit_part = jnp.stack(
        [
            jnp.sum(query_grad, (0, 1), dtype=jnp.float32),
            jnp.sum(value_grad, (0, 1), dtype=jnp.float32),
        ],
        1,
    )
    unit_part = jnp.concatenate(
        [unit_part, jnp.transpose(jnp.sum(up_low, (1, 2), dtype=jnp.float32))], 1
    )
    placed = lax.dynamic_update_slice_in_dim(
        jnp.zeros((MODEL_WIDTH, 6), jnp.float32), unit_part, tp_index * strip_width, 0
    )
    vector_part = jnp.concatenate([shared_part, placed], 1)
    input_red = lax.psum_scatter(
        input_part.astype(jnp.bfloat16), "tp", scatter_dimension=0, tiled=True
    ).astype(jnp.float32)
    block_local = all_blocks[0]
    input_grad = input_red + grad_one
    slot_dev = (12 + dp_count - 1) // dp_count
    padded = jnp.concatenate(
        [block_local, jnp.zeros((slot_dev * dp_count - 12, MODEL_WIDTH, strip_width), jnp.float32)],
        0,
    )
    block_grad, vector_owned = (
        lax.psum_scatter(padded.astype(jnp.bfloat16), "dp", scatter_dimension=0, tiled=True).astype(
            jnp.float32
        ),
        lax.psum_scatter(
            vector_part.astype(jnp.bfloat16), "dp", scatter_dimension=0, tiled=True
        ).astype(jnp.float32),
    )
    vector_grad = lax.psum(vector_owned, "tp")
    full_grad = lax.all_gather(block_grad.astype(jnp.bfloat16), "tp", axis=2, tiled=True).astype(
        block_grad.dtype
    )
    own_rows = lax.dynamic_slice_in_dim(full_grad, tp_index * strip_width, strip_width, 1)
    left_new = STAT_DECAY * left_stat + (1.0 - STAT_DECAY) * jnp.einsum(
        "sic,sjc->sij", own_rows, full_grad, precision=PRECISE
    )
    right_new = STAT_DECAY * right_stat + (1.0 - STAT_DECAY) * jnp.einsum(
        "sic,sij->scj", block_grad, full_grad, precision=PRECISE
    )
    precond = jnp.einsum("sij,sjc->sic", left_root, full_grad, precision=PRECISE)
    precond = jnp.einsum("sic,scj->sij", precond, right_root, precision=PRECISE)
    master_new = master - BLOCK_RATE * precond
    weight_copy = master_new.astype(jnp.bfloat16)
    ema_new = EMA_DECAY * averaged_weight + (1.0 - EMA_DECAY) * master_new
    owned_rows = vector_grad.shape[0]
    vector_rows = lax.dynamic_slice_in_dim(vectors, dp_index * owned_rows, owned_rows, 0)
    moment_new = MOMENTUM * vector_moment + vector_grad
    total_tokens = page_rows * seq_len * dp_count * tp_count
    vector_new = vector_rows - VEC_RATE * lax.rsqrt(jnp.float32(total_tokens)) * moment_new
    bias_grad = vector_grad[:, 0]
    return (
        layer_out,
        input_grad,
        block_grad,
        left_new,
        right_new,
        master_new,
        weight_copy,
        ema_new,
        vector_grad,
        moment_new,
        vector_new,
        bias_grad,
    )


def solution(mesh):
    return jax.shard_map(
        local,
        mesh=mesh,
        in_specs=(
            P(("dp", "tp"), None, None),
            P(("dp", "tp"), None),
            P(("dp", "tp"), None, None),
            P(("dp", "tp"), None, None),
            P(None, None, "tp"),
            P("tp", None),
            P(None, "tp", None),
            P(),
            P("dp", None),
            P("dp", "tp", None),
            P("dp", "tp", None),
            P("dp", "tp", None),
            P("dp", None, None),
            P("dp", "tp", None),
            P("dp", "tp", None),
        ),
        out_specs=(
            P(("dp", "tp"), None, None),
            P(("dp", "tp"), None, None),
            P("dp", None, "tp"),
            P("dp", "tp", None),
            P("dp", "tp", None),
            P("dp", "tp", None),
            P("dp", "tp", None),
            P("dp", "tp", None),
            P("dp", None),
            P("dp", None),
            P("dp", None),
            P("dp"),
        ),
        check_vma=False,
    )
```

profile of v0, /device:TPU:0, one launch (start us, length us, event | category | flops | bytes accessed | tf_op | source)
XLA Modules:
  0.0 1050.3 jit_solution(10930989319652648111)
XLA Ops:
  8.4 7.9 multiply_sine_fusion
  25.8 82.2 %all-gather.6.cloned.1.call-done = bf16[4,512,1024]{2,1,0:T(8,128)(2,1)} async-done(((bf16[1,512,1024]{2,1,0:T(8,128)(2,1)}), bf16[4,512,1024]{2,1,0:T(8,128)(2,1)}) %all-gather.6.cloned.1.call-update) | async-done | bytes 4194320 | tf_op jit(solution)/shard_map/all_gather | solution.py:144
  115.4 7.1 multiply_reduce_fusion.1
  122.5 8.6 exponential_reduce_fusion
  131.2 8.9 convolution_convert_fusion.2
  146.0 73.9 %reduce-scatter.9.cloned.1.call-done = bf16[1,512,1024]{2,1,0:T(8,128)(2,1)} async-done(((bf16[4,512,1024]{2,1,0:T(8,128)(2,1)}), bf16[1,512,1024]{2,1,0:T(8,128)(2,1)}) %reduce-scatter.9.cloned.1.call-update) | async-done | bytes 1048592 | tf_op jit(solution)/shard_map/reduce_scatter | solution.py:154
  225.7 80.7 %all-gather.8.cloned.1.call-done = bf16[4,512,1024]{2,1,0:T(8,128)(2,1)} async-done(((bf16[1,512,1024]{2,1,0:T(8,128)(2,1)}), bf16[4,512,1024]{2,1,0:T(8,128)(2,1)}) %all-gather.8.cloned.1.call-update) | async-done | bytes 4194320 | tf_op jit(solution)/shard_map/all_gather | solution.py:166
  306.4 26.1 %fusion.10 = (bf16[4,4,512,256]{3,2,0,1:T(8,128)(2,1)S(1)}, f32[4,4,512,256]{3,2,0,1:T(8,128)}, f32[4,512,4,256]{3,1,2,0:T(8,128)}) fusion(f32[4,256]{1,0:T(4,128)S(1)} %dynamic-slice_bitcast_fusion, bf16[7,1024,256]{2,1,0:T(8,128)(2,1)} %param.19, bf16[4,512,1024]{2,1,0:T(8,128)(2,1)} %all-gather.8.cloned.1.call-done), kind=kOutput, calls=%fused_computation.26 | convolution fusion | flops 4433379328 | bytes 27267072 | tf_op jit(solution)/shard_map/gtd,kdc->kgtc/dot_general | solution.py:167
  340.6 75.4 %reduce-scatter.11.cloned.1.call-done = bf16[1,512,1024]{2,1,0:T(8,128)(2,1)} async-done(((bf16[4,512,1024]{2,1,0:T(8,128)(2,1)}), bf16[1,512,1024]{2,1,0:T(8,128)(2,1)}) %reduce-scatter.11.cloned.1.call-update) | async-done | bytes 1048592 | tf_op jit(solution)/shard_map/reduce_scatter | solution.py:172
  423.9 81.2 %all-gather.10.cloned.1.call-done = bf16[4,512,1024]{2,1,0:T(8,128)(2,1)} async-done(((bf16[1,512,1024]{2,1,0:T(8,128)(2,1)}), bf16[4,512,1024]{2,1,0:T(8,128)(2,1)}) %all-gather.10.cloned.1.call-update) | async-done | bytes 4194320 | tf_op jit(solution)/shard_map/all_gather | solution.py:186
  505.0 13.5 %convert_reduce_fusion = (bf16[4,256]{1,0:T(4,128)(2,1)}, bf16[4,4,512,256]{3,2,0,1:T(8,128)(2,1)S(1)}) fusion(f32[4,4,512,256]{3,2,0,1:T(8,128)} %get-tuple-element.67, bf16[4,256,1024]{2,1,0:T(8,128)(2,1)S(1)} %copy-done, bf16[4,512,1024]{2,1,0:T(8,128)(2,1)} %all-gather.10.cloned.1.call-done, f32[4,512,4,256]{3,1,2,0:T(8,128)} %get-tuple-element.85, ...), kind=kOutput, calls=%fused_computation.27 | convolution fusion | flops 4330617856 | bytes 27269120 | tf_op jit(solution)/shard_map/gtd,kcd->kgtc/dot_general | solution.py:187
  527.0 75.4 %reduce-scatter.13.cloned.1.call-done = bf16[1,512,1024]{2,1,0:T(8,128)(2,1)} async-done(((bf16[4,512,1024]{2,1,0:T(8,128)(2,1)}), bf16[1,512,1024]{2,1,0:T(8,128)(2,1)}) %reduce-scatter.13.cloned.1.call-update) | async-done | bytes 1048592 | tf_op jit(solution)/shard_map/reduce_scatter | solution.py:190
  610.1 9.5 fusion.45
  625.5 65.9 %all-gather.12.cloned.1.call-done = bf16[4,512,1024]{2,1,0:T(8,128)(2,1)} async-done(((bf16[1,512,1024]{2,1,0:T(8,128)(2,1)}), bf16[4,512,1024]{2,1,0:T(8,128)(2,1)}) %all-gather.12.cloned.1.call-update) | async-done | bytes 4194320 | tf_op jit(solution)/shard_map/all_gather | solution.py:202
  694.9 7.7 convert_reduce_fusion.1
  702.7 11.2 %multiply_reduce_fusion = (f32[4,4,512]{2,1,0:T(4,128)S(1)}, f32[4,4,512,512]{2,3,1,0:T(8,128)}) fusion(f32[4,4,512,512]{2,3,1,0:T(8,128)} %get-tuple-element.84, f32[4,4,512]{2,1,0:T(4,128)S(1)} %bitcast.268, bf16[4,512,4,64]{1,3,2,0:T(8,128)(2,1)S(1)} %bitcast.260, f32[4,512,4,64]{1,3,2,0:T(8,128)S(1)} %bitcast.254, f32[4,64]{1,0:T(4,128)S(1)} %copy-done.38), kind=kOutput, calls=%fused_computation.1 | convolution fusion | flops 554688512 | bytes 36766720 | tf_op jit(solution)/shard_map/gqhe,gkhe->ghqk/dot_general | solution.py:96
  713.9 12.7 %multiply_convert_fusion = bf16[4,4,512,512]{2,3,1,0:T(8,128)(2,1)S(1)} fusion(f32[4,4,512,512]{2,3,1,0:T(8,128)} %get-tuple-element.87, f32[4,4,512,512]{2,3,1,0:T(8,128)} %get-tuple-element.84, f32[4,4,512]{2,1,0:T(4,128)S(1)} %get-tuple-element.86, f32[4,4,512]{2,1,0:T(4,128)S(1)} %bitcast.269), kind=kLoop, calls=%fused_computation | loop fusion | flops 20971520 | bytes 42008576 | tf_op jit(solution)/shard_map/convert_element_type | solution.py:99
  754.1 7.9 bitcast_convert_fusion
  762.1 59.2 %reduce-scatter.17.cloned.1.call-done = bf16[2,1024,256]{1,2,0:T(8,128)(2,1)} async-done(((bf16[16,1024,256]{1,2,0:T(8,128)(2,1)}), bf16[2,1024,256]{1,2,0:T(8,128)(2,1)}) %reduce-scatter.17.cloned.1.call-update) | async-done | bytes 1048592 | tf_op jit(solution)/shard_map/reduce_scatter | solution.py:268
  821.3 37.2 %reduce-scatter.19.cloned.1.call-done = bf16[128,12]{1,0:T(8,128)(2,1)} async-done(((bf16[1024,12]{1,0:T(8,128)(2,1)}), bf16[128,12]{1,0:T(8,128)(2,1)}) %reduce-scatter.19.cloned.1.call-update) | async-done | bytes 3088
  859.3 12.1 %psum.7 = f32[128,12]{0,1:T(8,128)S(1)} all-reduce(bf16[128,12]{0,1:T(8,128)(2,1)S(1)} %copy.126), channel_id=1, replica_groups=mesh['dp'=8,'tp'=4] {'tp'}, use_global_device_ids=true, to_apply=%region_26.0 | all-reduce | flops 1536 | bytes 9216 | tf_op jit(solution)/shard_map/psum | solution.py:275
  873.2 64.4 %reduce-scatter.15.cloned.1.call-done = bf16[1,512,1024]{2,1,0:T(8,128)(2,1)} async-done(((bf16[4,512,1024]{2,1,0:T(8,128)(2,1)}), bf16[1,512,1024]{2,1,0:T(8,128)(2,1)}) %reduce-scatter.15.cloned.1.call-update) | async-done | bytes 1048592 | tf_op jit(solution)/shard_map/reduce_scatter | solution.py:257
  942.4 78.0 %all-gather.14.cloned.1.call-done = bf16[2,1024,1024]{1,2,0:T(8,128)(2,1)} async-done(((bf16[2,1024,256]{1,2,0:T(8,128)(2,1)}), bf16[2,1024,1024]{1,2,0:T(8,128)(2,1)}) %all-gather.14.cloned.1.call-update) | async-done | bytes 4194320 | tf_op jit(solution)/shard_map/all_gather | solution.py:276
  1026.8 11.5 %multiply_add_fusion = (f32[2,256,1024]{2,1,0:T(8,128)}, bf16[2,256,1024]{2,1,0:T(8,128)(2,1)}, f32[2,256,1024]{2,1,0:T(8,128)}) fusion(f32[2,256,1024]{2,1,0:T(8,128)S(1)} %copy-done.23, f32[2,256,1024]{2,1,0:T(8,128)S(1)} %copy-done.24, f32[2,1024,256]{1,2,0:T(8,128)S(1)} %fusion.97, f32[2,1024,1024]{2,1,0:T(8,128)} %param.27), kind=kOutput, calls=%fused_computation.79 | convolution fusion | flops 6445596672 | bytes 19922944 | tf_op jit(solution)/shard_map/sic,scj->sij/dot_general | solution.py:287
  (198 shorter events, 117.4 us)
Async XLA Ops:
  7.2 327.2 %copy-start = (bf16[4,256,1024]{2,1,0:T(8,128)(2,1)S(1)}, bf16[4,256,1024]{2,1,0:T(8,128)(2,1)}, u32[]{:S(2)}) copy-start(bf16[4,256,1024]{2,1,0:T(8,128)(2,1)} %param.21) | copy-start | bytes 6291460
  7.2 100.9 %all-gather.6.cloned.1.call-start = ((), (), s32[]{:S(2)}) async-start(), calls=%async_computation.6 | async-start | bytes 5242880 | tf_op jit(solution)/shard_map/all_gather | solution.py:144
  24.4 195.4 %reduce-scatter.9.cloned.1.call-start = ((), (), s32[]{:S(2)}) async-start(), calls=%async_computation.7 | async-start | bytes 5242880 | tf_op jit(solution)/shard_map/reduce_scatter | solution.py:154
  25.7 105.4 %copy-start.37 = (f32[4,64]{1,0:T(4,128)}, f32[4,64]{1,0:T(4,128)S(1)}, u32[]{:S(2)}) copy-start(f32[4,64]{1,0:T(4,128)S(1)} %add.150) | copy-start | bytes 3076
  25.8 89.1 %copy-start.40 = (f32[4,64]{1,0:T(4,128)}, f32[4,64]{1,0:T(4,128)S(1)}, u32[]{:S(2)}) copy-start(f32[4,64]{1,0:T(4,128)S(1)} %add.153) | copy-start | bytes 3076
  114.9 16.2 %copy-start.5 = (f32[1,4,512,256]{2,3,0,1:T(8,128)}, f32[1,4,512,256]{2,3,0,1:T(8,128)S(1)}, u32[]{:S(2)}) copy-start(f32[1,4,512,256]{2,3,0,1:T(8,128)S(1)} %get-tuple-element.70) | copy-start | bytes 6291460
  141.1 78.7 %copy-start.19 = (bf16[1,512,1024]{2,1,0:T(8,128)(2,1)S(1)}, bf16[1,512,1024]{2,1,0:T(8,128)(2,1)}, u32[]{:S(2)}) copy-start(bf16[1,512,1024]{2,1,0:T(8,128)(2,1)} %param.15) | copy-start | bytes 3145732
  144.4 162.0 %all-gather.8.cloned.1.call-start = ((), (), s32[]{:S(2)}) async-start(), calls=%async_computation.8 | async-start | bytes 5242880 | tf_op jit(solution)/shard_map/all_gather | solution.py:166
  225.0 191.0 %reduce-scatter.11.cloned.1.call-start = ((), (), s32[]{:S(2)}) async-start(), calls=%async_computation.9 | async-start | bytes 5242880 | tf_op jit(solution)/shard_map/reduce_scatter | solution.py:172
  340.5 78.5 %copy-start.15 = (bf16[1,512,1024]{2,1,0:T(8,128)(2,1)S(1)}, bf16[1,512,1024]{2,1,0:T(8,128)(2,1)}, u32[]{:S(2)}) copy-start(bf16[1,512,1024]{2,1,0:T(8,128)(2,1)} %param.18) | copy-start | bytes 3145732
  340.5 164.5 %all-gather.10.cloned.1.call-start = ((), (), s32[]{:S(2)}) async-start(), calls=%async_computation.10 | async-start | bytes 5242880 | tf_op jit(solution)/shard_map/all_gather | solution.py:186
  423.6 178.8 %reduce-scatter.13.cloned.1.call-start = ((), (), s32[]{:S(2)}) async-start(), calls=%async_computation.11 | async-start | bytes 5242880 | tf_op jit(solution)/shard_map/reduce_scatter | solution.py:190
  526.9 75.5 %copy-start.3 = (f32[1,512,1024]{2,1,0:T(8,128)S(1)}, f32[1,512,1024]{2,1,0:T(8,128)}, u32[]{:S(2)}) copy-start(f32[1,512,1024]{2,1,0:T(8,128)} %copy-done.2) | copy-start | bytes 6291460
  526.9 164.5 %all-gather.12.cloned.1.call-start = ((), (), s32[]{:S(2)}) async-start(), calls=%async_computation.12 | async-start | bytes 5242880 | tf_op jit(solution)/shard_map/all_gather | solution.py:202
  610.0 211.3 %reduce-scatter.17.cloned.1.call-start = ((), (), s32[]{:S(2)}) async-start(), calls=%async_computation.14 | async-start | bytes 9437184 | tf_op jit(solution)/shard_map/reduce_scatter | solution.py:268
  619.5 71.9 %copy-start.36 = (bf16[256,1024]{1,0:T(8,128)(2,1)S(1)}, bf16[256,1024]{1,0:T(8,128)(2,1)}, u32[]{:S(2)}) copy-start(bf16[256,1024]{1,0:T(8,128)(2,1)} %param.20) | copy-start | bytes 1572868
  625.5 69.4 %copy-start.34 = (f32[2,8,512]{2,1,0:T(8,128)S(1)}, f32[2,8,512]{2,1,0:T(8,128)}, u32[]{:S(2)}) copy-start(f32[2,8,512]{2,1,0:T(8,128)} %copy-done.33) | copy-start | bytes 98308
  751.3 107.2 %reduce-scatter.19.cloned.1.call-start = ((), (), s32[]{:S(2)}) async-start(), calls=%async_computation.16 | async-start | bytes 294912
  754.0 183.6 %reduce-scatter.15.cloned.1.call-start = ((), (), s32[]{:S(2)}) async-start(), calls=%async_computation.13 | async-start | bytes 5242880 | tf_op jit(solution)/shard_map/reduce_scatter | solution.py:257
  762.0 109.9 %copy-start.46 = (f32[128,12]{0,1:T(8,128)S(1)}, f32[128,12]{0,1:T(8,128)}, u32[]{:S(2)}) copy-start(f32[128,12]{0,1:T(8,128)} %param.23) | copy-start | bytes 18436
  762.0 175.7 %copy-start.8 = (f32[1,512,1024]{2,1,0:T(8,128)S(1)}, f32[1,512,1024]{2,1,0:T(8,128)}, u32[]{:S(2)}) copy-start(f32[1,512,1024]{2,1,0:T(8,128)} %copy-done.7) | copy-start | bytes 6291460
  762.0 258.4 %all-gather.14.cloned.1.call-start = ((), (), s32[]{:S(2)}) async-start(), calls=%async_computation.15 | async-start | bytes 5242880 | tf_op jit(solution)/shard_map/all_gather | solution.py:276
  821.3 119.3 %copy-start.12 = (bf16[2,1024,256]{1,2,0:T(8,128)(2,1)S(1)}, bf16[2,1024,256]{1,2,0:T(8,128)(2,1)}, u32[]{:S(2)}) copy-start(bf16[2,1024,256]{1,2,0:T(8,128)(2,1)} %reduce-scatter.17.cloned.1.call-done) | copy-start | bytes 3145732
  871.4 71.0 %copy-start.39 = (f32[128,12]{0,1:T(8,128)}, f32[128,12]{0,1:T(8,128)S(1)}, u32[]{:S(2)}) copy-start(f32[128,12]{0,1:T(8,128)S(1)} %psum.7) | copy-start | bytes 18436
  (42 other events, 214.6 us)
Sparse Core Ops, SparseCore 0:
  24.6 83.4 all-gather.5
  144.5 75.2 reduce-scatter.8
  225.1 81.2 all-gather.7
  340.6 75.2 reduce-scatter.10
  423.8 81.2 all-gather.9
  527.1 75.2 reduce-scatter.12
  610.1 81.2 all-gather.11
  751.4 69.8 reduce-scatter.16
  824.9 33.5 reduce-scatter.18
  860.8 76.8 reduce-scatter.14
  939.2 81.1 all-gather.13
where the time goes:
time: 1050 us
  waiting for transfers between devices  774 us (74%)
  matrix products  161 us (15%)
  other arithmetic  57.5 us (5%)
  local copies, waits for them, and re-layouts  30.1 us (3%)
  between operations  14.7 us (1%)
  blocking collectives  12.1 us (1%)
    all_gather x1, waiting for transfers between devices, local(): x_input = lax.all_gather(x_low, 'tp', axis=0, tiled=True)  82.2 us
    all_gather x1, waiting for transfers between devices, local(): two_input = lax.all_gather(two_low, 'tp', axis=0, tiled=True)  81.2 us
    all_gather x1, waiting for transfers between devices, local(): mid_input = lax.all_gather(mid_low, 'tp', axis=0, tiled=True)  80.7 us
    all_gather x1, waiting for transfers between devices, local(): lax.all_gather(block_grad.astype(jnp.bfloat16), 'tp', axis=2, tiled=True)  78 us
    reduce_scatter x1, waiting for transfers between devices, local(): lax.psum_scatter(jnp.einsum('kgtc,kdc->gtd', up_low, col_mats[3:7], prefe...  75.4 us
    reduce_scatter x1, waiting for transfers between devices, local(): lax.psum_scatter(jnp.einsum('kgtc,kcd->gtd', act_low, down_mats, preferre...  75.4 us
    reduce_scatter x1, waiting for transfers between devices, local(): lax.psum_scatter(jnp.einsum('gtc,cd->gtd', context, out_mat, preferred_el...  73.9 us
    all_gather x1, waiting for transfers between devices, local(): one_input = lax.all_gather(one_low, 'tp', axis=0, tiled=True)  65.9 us
  transfers between devices with their start and end apart: 11, of which 11 were waited for; matrix products, arithmetic and copies ran while one was open for 3% of the time, Pallas kernels for 0%

commit v1 on v0

--- a/solution.py
+++ b/solution.py
@@ -3,12 +3,13 @@
 import jax
 import jax.numpy as jnp
 from jax import lax
+from jax.experimental import pallas as pl
+from jax.experimental.pallas import tpu as pltpu
 from jax.sharding import PartitionSpec as P
 
 MODEL_WIDTH = 1024
 H = 16
 HD = 64
-
 
 PRECISE = lax.Precision.HIGHEST
 EPS_NORM = 1e-06
@@ -17,6 +18,563 @@
 EMA_DECAY = 0.9
 MOMENTUM = 0.9
 VEC_RATE = 0.2
+
+MESH = pl.DeviceIdType.MESH
+
+
+def position():
+    d, z = lax.axis_index("dp"), lax.axis_index("tp")
+    core, x, y = d % 2, (d // 2) % 2, d // 4
+    near = {
+        "x": (d + 2 - 4 * x, z),
+        "y": (d + 4 - 8 * y, z),
+        "c": (d + 1 - 2 * core, z),
+        "u": (d, z + 1),
+        "v": (d, z - 1),
+    }
+    return z, core, x, y, near
+
+
+def meet(z, near, extra=()):
+    barrier = pltpu.get_barrier_semaphore()
+    always = [near[name] for name in "xyc"] + list(extra)
+    for device in always:
+        pl.semaphore_signal(barrier, 1, device_id=device, device_id_type=MESH)
+
+    @pl.when(z < 3)
+    def _():
+        pl.semaphore_signal(barrier, 1, device_id=near["u"], device_id_type=MESH)
+
+    @pl.when(z > 0)
+    def _():
+        pl.semaphore_signal(barrier, 1, device_id=near["v"], device_id_type=MESH)
+
+    pl.semaphore_wait(barrier, len(always) + (z + 2) // 3 + (5 - z) // 3)
+
+
+ORDER = (0, 1, 2, 7, 3, 4, 5, 6, 8, 9, 10, 11)
+
+
+def gather_kernel(
+    cols, outw, down, full, bounce_cols, bounce_rows, load, store, along, onward, arrived, beside
+):
+    z, core, x, y, near = position()
+    p = 2 * y + x
+    meet(z, near)
+
+    def own(k, h):
+        if k < 7:
+            return cols.at[k, pl.ds(h * 512, 512), :]
+        if k == 7:
+            return outw.at[pl.ds(h * 128, 128), :]
+        return down.at[k - 8, pl.ds(h * 128, 128), :]
+
+    def spot(s, k, h):
+        if k < 7:
+            return full.at[k, pl.ds(h * 512, 512), pl.ds(pl.multiple_of(s * 256, 256), 256)]
+        return full.at[k, pl.ds(pl.multiple_of(s * 256 + h * 128, 128), 128), :]
+
+    def spot_whole(s, k):
+        if k < 7:
+            return full.at[k, :, pl.ds(pl.multiple_of(s * 256, 256), 256)]
+        return full.at[k, pl.ds(pl.multiple_of(s * 256, 256), 256), :]
+
+    def to(source, s, k, send_sem, recv_sem, name):
+        return pltpu.make_async_remote_copy(
+            src_ref=source,
+            dst_ref=spot(s, k, core),
+            send_sem=send_sem,
+            recv_sem=recv_sem.at[s, k],
+            device_id=near[name],
+            device_id_type=MESH,
+        )
+
+    def first(g, act):
+        for t in range(3):
+            k = ORDER[3 * g + t]
+            mine = (p == t) | (p == 3) if t == 0 else p == t
+
+            @pl.when(mine & (z < 3))
+            def _(k=k):
+                act(to(own(k, core), z, k, along.at[k], arrived, "u"))
+
+            @pl.when(mine & (z > 0))
+            def _(k=k):
+                act(to(own(k, core), z, k, onward.at[0, z, k], arrived, "v"))
+
+    far = 3 * (1 - z // 2)
+    nearest = z + 1 - 2 * (z // 3)
+    strips = (nearest, 6 - nearest - far - z, far)
+
+    def item(n, t):
+        return strips[n % 3], ORDER[3 * (n // 3) + t]
+
+    first(0, lambda copy: copy.start())
+    first(1, lambda copy: copy.start())
+    for k in ORDER:
+        if k < 7:
+            pltpu.make_async_copy(cols.at[k], bounce_cols.at[k], load.at[k]).start()
+        else:
+            source = outw if k == 7 else down.at[k - 8]
+            pltpu.make_async_copy(source, bounce_rows.at[k - 7], load.at[k]).start()
+
+    def bounce(k, act):
+        if k < 7:
+            act(pltpu.make_async_copy(bounce_cols.at[k], spot_whole(z, k), store.at[k]))
+        else:
+            act(pltpu.make_async_copy(bounce_rows.at[k - 7], spot_whole(z, k), store.at[k]))
+
+    def go(s, k, kind, name, sems):
+        return to(spot(s, k, core), s, k, onward.at[kind, s, k], sems, name)
+
+    def stage(n, hop, begin):
+        for t in range(3):
+            s, k = item(n, t)
+            who = {
+                (0, 0): (p == 0) | (p == 3),
+                (0, 1): p == 1,
+                (0, 2): p == 2,
+                (1, 0): (p == 1) | (p == 2),
+                (1, 1): (p == 0) | (p == 3),
+                (1, 2): (p == 0) | (p == 3),
+                (2, 0): None,
+                (2, 1): p == 2,
+                (2, 2): p == 1,
+            }[hop, t]
+            if who is None:
+                continue
+
+            @pl.when(who)
+            def _(s=s, k=k, t=t):
+                if begin:
+                    go(s, k, 0, "x", arrived).wait_recv()
+
+                def act(copy):
+                    if begin:
+                        copy.start()
+                    else:
+                        copy.wait_send()
+
+                if hop == 0:
+
+                    @pl.when((s > z) & (z > 0))
+                    def _():
+                        act(go(s, k, 0, "v", arrived))
+
+                    @pl.when((s < z) & (z < 3))
+                    def _():
+                        act(go(s, k, 0, "u", arrived))
+
+                    if t == 0:
+
+                        @pl.when(p == 0)
+                        def _():
+                            act(go(s, k, 1, "x", arrived))
+                            act(go(s, k, 2, "y", arrived))
+                    else:
+                        act(go(s, k, 1, "x", arrived))
+                        act(go(s, k, 2, "y", arrived))
+                if hop == 1 and t == 1:
+
+                    @pl.when(p == 3)
+                    def _():
+                        act(go(s, k, 1, "x", arrived))
+
+                if hop == 1 and t == 2:
+
+                    @pl.when(p == 3)
+                    def _():
+                        act(go(s, k, 2, "y", arrived))
+
+                act(go(s, k, 3, "c", beside))
+
+    for n in range(14):
+        if n in (3, 6):
+            first(n // 3 + 1, lambda copy: copy.start())
+        if n == 2:
+            for k in ORDER:
+                if k < 7:
+                    pltpu.make_async_copy(cols.at[k], bounce_cols.at[k], load.at[k]).wait()
+                else:
+                    source = outw if k == 7 else down.at[k - 8]
+                    pltpu.make_async_copy(source, bounce_rows.at[k - 7], load.at[k]).wait()
+                bounce(k, lambda copy: copy.start())
+        for hop in range(3):
+            if 0 <= n - hop < 12:
+                stage(n - hop, hop, True)
+    for n in range(12):
+        for hop in range(3):
+            stage(n, hop, False)
+        for t in range(3):
+            s, k = item(n, t)
+            pltpu.make_async_remote_copy(
+                src_ref=spot(s, k, 1 - core),
+                dst_ref=spot(s, k, 1 - core),
+                send_sem=onward.at[3, s, k],
+                recv_sem=beside.at[s, k],
+                device_id=near["c"],
+                device_id_type=MESH,
+            ).wait_recv()
+    for g in range(4):
+        first(g, lambda copy: copy.wait_send())
+    for k in ORDER:
+        bounce(k, lambda copy: copy.wait())
+
+
+def gather_weights(cols, outw, down):
+    anywhere = pl.BlockSpec(memory_space=pl.ANY)
+    dma = pltpu.SemaphoreType.DMA
+    return pl.pallas_call(
+        gather_kernel,
+        name="gather_weights",
+        out_shape=jax.ShapeDtypeStruct((12, MODEL_WIDTH, MODEL_WIDTH), jnp.bfloat16),
+        in_specs=[anywhere] * 3,
+        out_specs=anywhere,
+        scratch_shapes=[
+            pltpu.VMEM((7, 1024, 256), jnp.bfloat16),
+            pltpu.VMEM((5, 256, 1024), jnp.bfloat16),
+            dma((12,)),
+            dma((12,)),
+            dma((12,)),
+            dma((4, 4, 12)),
+            dma((4, 12)),
+            dma((4, 12)),
+        ],
+        compiler_params=pltpu.CompilerParams(
+            collective_id=1, has_side_effects=True, vmem_limit_bytes=16 << 20
+        ),
+    )(cols, outw, down)
+
+
+CHUNK = 64
+STEPS = 2 * (MODEL_WIDTH // CHUNK)
+PER_SLOT = MODEL_WIDTH // CHUNK
+
+
+def reduce_kernel(
+    qkv, up, outb, down, vec, total, vec_sum,
+    mine, sibling, merged, side, chain, vec_in,
+    load, cross_send, cross_recv, send, merge_recv, side_recv, chain_send, chain_recv, vec_send, vec_recv,
+):
+    z, core, x, y, near = position()
+    p = 2 * y + x
+    d = 2 * p + core
+    z_one = (d, z + 1 - 2 * (z % 2))
+    z_two = (d, z + 2 - 4 * (z // 2))
+    meet(z, near, (z_two,))
+
+    def block(slot):
+        if slot < 3:
+            return qkv.at[slot]
+        if slot < 7:
+            return up.at[slot - 3]
+        if slot == 7:
+            return outb.at[0]
+        return down.at[slot - 8]
+
+    order = [(i, j) for i in range(2) for j in (2, 1, 0)]
+
+    def fetch(j, i, c):
+        return pltpu.make_async_copy(block((2 * j + c) * 2 + i), mine.at[2 * j + i], load.at[2 * j + i])
+
+    def give(j, i, c, q):
+        return pltpu.make_async_remote_copy(
+            src_ref=block((2 * j + c) * 2 + i).at[pl.ds(q * 256, 256), :],
+            dst_ref=sibling.at[2 * j + i, pl.ds(q * 256, 256), :],
+            send_sem=cross_send.at[2 * j + i, q],
+            recv_sem=cross_recv.at[2 * j + i, q],
+            device_id=near["c"],
+            device_id_type=MESH,
+        )
+
+    for c in range(2):
+
+        @pl.when(core == c)
+        def _(c=c):
+            for i, j in order:
+                fetch(j, i, c).start()
+                for q in range(4):
+                    give(j, i, 1 - c, q).start()
+
+    def vec_hop(h):
+        device = (near["c"], near["x"], near["y"], z_one, z_two)[h]
+        return pltpu.make_async_remote_copy(
+            src_ref=vec_sum,
+            dst_ref=vec_in.at[h],
+            send_sem=vec_send.at[h],
+            recv_sem=vec_recv.at[h],
+            device_id=device,
+            device_id_type=MESH,
+        )
+
+    vec_sum[...] = vec[...]
+    vec_hop(0).start()
+
+    @pl.when(p == 3)
+    def _():
+        total[...] = jnp.zeros_like(total)
+
+    def rows(r):
+        return pl.ds(pl.multiple_of(r * CHUNK, CHUNK), CHUNK)
+
+    def remote(source, dest, send_sem, recv_sem, device):
+        return pltpu.make_async_remote_copy(
+            src_ref=source, dst_ref=dest, send_sem=send_sem, recv_sem=recv_sem,
+            device_id=device, device_id_type=MESH,
+        )
+
+    def forward(s, i, r, place, name, act):
+        act(remote(mine.at[s, rows(r), :], side.at[place, i, rows(r), :], send.at[s, r], side_recv.at[place, i * PER_SLOT + r], near[name]))
+
+    def to_merge(s, r, name, act):
+        act(remote(mine.at[s, rows(r), :], merged.at[s, rows(r), :], send.at[s, r], merge_recv.at[s, r], near[name]))
+
+    def roles(j):
+        rx = x if j % 2 == 0 else 1 - x
+        ry = y if j // 2 == 0 else 1 - y
+        return rx, ry
+
+    def add(ref_a, ref_b):
+        return ref_a[...].astype(jnp.float32) + ref_b[...].astype(jnp.float32)
+
+    def sends(j, i, r, act, direct):
+        s = 2 * j + i
+        rx, ry = roles(j)
+        if direct:
+
+            @pl.when((rx == 1) & (ry == 1) & (r % 2 == 0))
+            def _():
+                to_merge(s, r, "x", act)
+
+            @pl.when((rx == 1) & (ry == 1) & (r % 2 == 1))
+            def _():
+                to_merge(s, r, "y", act)
+
+            @pl.when((rx == 1) & (ry == 0) & (r % 2 == 0))
+            def _():
+                forward(s, i, r, 0, "x", act)
+
+            @pl.when((rx == 0) & (ry == 1) & (r % 2 == 1))
+            def _():
+                forward(s, i, r, 1, "y", act)
+        else:
+
+            @pl.when((rx == 1) & (ry == 0) & (r % 2 == 1))
+            def _():
+                forward(s, i, r, 0, "x", act)
+
+            @pl.when((rx == 0) & (ry == 1) & (r % 2 == 0))
+            def _():
+                forward(s, i, r, 1, "y", act)
+
+    begin = lambda copy: copy.start()
+
+    def stage_one(m):
+        i, r = m // PER_SLOT, m % PER_SLOT
+        for j in (2, 1, 0):
+            s = 2 * j + i
+
+            @pl.when(r == 0)
+            def _(s=s):
+                pltpu.make_async_copy(down.at[0], mine.at[s], load.at[s]).wait()
+
+            @pl.when(r % 4 == 0)
+            def _(s=s):
+                q = r // 4
+                remote(
+                    sibling.at[s, pl.ds(pl.multiple_of(q * 256, 256), 256), :],
+                    sibling.at[s, pl.ds(pl.multiple_of(q * 256, 256), 256), :],
+                    cross_send.at[s, q], cross_recv.at[s, q], near["c"],
+                ).wait_recv()
+
+            mine[s, rows(r), :] = add(mine.at[s, rows(r), :], sibling.at[s, rows(r), :]).astype(jnp.bfloat16)
+            sends(j, i, r, begin, True)
+
+    def stage_two(m):
+        i, r = m // PER_SLOT, m % PER_SLOT
+        for j in (2, 1, 0):
+            s = 2 * j + i
+            rx, ry = roles(j)
+
+            @pl.when(((rx == 1) & (ry == 0) & (r % 2 == 1)) | ((rx == 0) & (ry == 1) & (r % 2 == 0)))
+            def _(s=s):
+                remote(merged.at[s, rows(r), :], merged.at[s, rows(r), :], send.at[s, r], merge_recv.at[s, r], near["x"]).wait_recv()
+                mine[s, rows(r), :] = add(mine.at[s, rows(r), :], merged.at[s, rows(r), :]).astype(jnp.bfloat16)
+
+            sends(j, i, r, begin, False)
+
+    def pass_on(m, way, act):
+        i, r = m // PER_SLOT, m % PER_SLOT
+        def copy(source, name):
+            return remote(source, chain.at[way, i, rows(r), :], chain_send.at[way, m], chain_recv.at[way, m], near[name])
+        name = "u" if way == 0 else "v"
+        end = 0 if way == 0 else 3
+
+        @pl.when(z == end)
+        def _():
+            act(copy(mine.at[2 * p + i, rows(r), :], name))
+
+        @pl.when((z == 1) | (z == 2))
+        def _():
+            act(copy(side.at[way, i, rows(r), :], name))
+
+    def stage_three(m):
+        i, r = m // PER_SLOT, m % PER_SLOT
+        s = 2 * p + i
+        for place in range(2):
+            remote(side.at[place, i, rows(r), :], side.at[place, i, rows(r), :], send.at[s, r], side_recv.at[place, m], near["x"]).wait_recv()
+        value = add(mine.at[s, rows(r), :], side.at[0, i, rows(r), :]) + side[1, i, rows(r), :].astype(jnp.float32)
+        mine[s, rows(r), :] = value.astype(jnp.bfloat16)
+
+        @pl.when(z == 0)
+        def _():
+            pass_on(m, 0, begin)
+
+        @pl.when(z == 3)
+        def _():
+            pass_on(m, 1, begin)
+
+    def chain_in(m, way):
+        i, r = m // PER_SLOT, m % PER_SLOT
+        remote(chain.at[way, i, rows(r), :], chain.at[way, i, rows(r), :], chain_send.at[way, m], chain_recv.at[way, m], near["x"]).wait_recv()
+
+    def link(m, way, last):
+        i, r = m // PER_SLOT, m % PER_SLOT
+        s = 2 * p + i
+        chain_in(m, way)
+        side[way, i, rows(r), :] = add(mine.at[s, rows(r), :], chain.at[way, i, rows(r), :]).astype(jnp.bfloat16)
+        pass_on(m, way, begin)
+        if last:
+            total[i, rows(r), :] = add(side.at[1 - way, i, rows(r), :], chain.at[way, i, rows(r), :]).astype(jnp.bfloat16)
+
+    def stage_four(m):
+        @pl.when(z == 1)
+        def _():
+            link(m, 0, False)
+
+        @pl.when(z == 2)
+        def _():
+            link(m, 1, False)
+
+    def stage_five(m):
+        @pl.when(z == 1)
+        def _():
+            link(m, 1, True)
+
+        @pl.when(z == 2)
+        def _():
+            link(m, 0, True)
+
+    def stage_six(m):
+        i, r = m // PER_SLOT, m % PER_SLOT
+        s = 2 * p + i
+        for end, way in ((0, 1), (3, 0)):
+
+            @pl.when(z == end)
+            def _(way=way):
+                chain_in(m, way)
+                total[i, rows(r), :] = add(mine.at[s, rows(r), :], chain.at[way, i, rows(r), :]).astype(jnp.bfloat16)
+
+    lags = LAGS
+
+    def step(n, carry):
+        @pl.when(n < STEPS)
+        def _():
+            stage_one(n)
+
+        m2 = n - lags[0]
+
+        @pl.when((m2 >= 0) & (m2 < STEPS))
+        def _():
+            stage_two(m2)
+
+        for lag, stage in zip(lags[1:], (stage_three, stage_four, stage_five, stage_six)):
+            m = n - lag
+
+            @pl.when((m >= 0) & (m < STEPS) & (p < 3))
+            def _(m=m, stage=stage):
+                stage(m)
+
+        for h in range(5):
+
+            @pl.when(n == 2 + 3 * h)
+            def _(h=h):
+                vec_hop(h).wait()
+                vec_sum[...] = vec_sum[...] + vec_in[h]
+                if h < 4:
+                    vec_hop(h + 1).start()
+
+        return carry
+
+    lax.fori_loop(0, STEPS + lags[4], step, 0)
+
+    for c in range(2):
+
+        @pl.when(core == c)
+        def _(c=c):
+            for i, j in order:
+                for q in range(4):
+                    give(j, i, 1 - c, q).wait_send()
+
+    def finish(m, carry):
+        i, r = m // PER_SLOT, m % PER_SLOT
+        end = lambda copy: copy.wait_send()
+        for j in range(3):
+            sends(j, i, r, end, True)
+            sends(j, i, r, end, False)
+
+        @pl.when((p < 3) & (z < 3))
+        def _():
+            pass_on(m, 0, end)
+
+        @pl.when((p < 3) & (z > 0))
+        def _():
+            pass_on(m, 1, end)
+
+        return carry
+
+    lax.fori_loop(0, STEPS, finish, 0)
+
+
+LAGS = (2, 4, 6, 8, 10)
+
+
+def reduce_blocks(qkv, up, outb, down, vec):
+    anywhere = pl.BlockSpec(memory_space=pl.ANY)
+    vmem = pl.BlockSpec(memory_space=pltpu.VMEM)
+    dma = pltpu.SemaphoreType.DMA
+    wide = MODEL_WIDTH
+    return pl.pallas_call(
+        reduce_kernel,
+        name="reduce_blocks",
+        out_shape=(
+            jax.ShapeDtypeStruct((2, wide, wide), jnp.bfloat16),
+            jax.ShapeDtypeStruct(vec.shape, jnp.float32),
+        ),
+        in_specs=[anywhere] * 4 + [vmem],
+        out_specs=(vmem, vmem),
+        scratch_shapes=[
+            pltpu.VMEM((6, wide, wide), jnp.bfloat16),
+            pltpu.VMEM((6, wide, wide), jnp.bfloat16),
+            pltpu.VMEM((6, wide, wide), jnp.bfloat16),
+            pltpu.VMEM((2, 2, wide, wide), jnp.bfloat16),
+            pltpu.VMEM((2, 2, wide, wide), jnp.bfloat16),
+            pltpu.VMEM((5,) + vec.shape, jnp.float32),
+            dma((6,)),
+            dma((6, 4)),
+            dma((6, 4)),
+            dma((6, PER_SLOT)),
+            dma((6, PER_SLOT)),
+            dma((2, STEPS)),
+            dma((2, STEPS)),
+            dma((2, STEPS)),
+            dma((5,)),
+            dma((5,)),
+        ],
+        compiler_params=pltpu.CompilerParams(
+            collective_id=2, has_side_effects=True, vmem_limit_bytes=62 << 20
+        ),
+    )(qkv, up, outb, down, vec)
 
 
 def layout_embed(cell_boxes, cell_ids):
@@ -138,98 +696,71 @@
     dp_index = lax.axis_index("dp")
     strip_width = weight_cols.shape[2]
     page_rows, seq_len = (hidden.shape[0], hidden.shape[1])
+    near_plan = dp_count == 8 and tp_count == 4
+    if near_plan:
+        full = gather_weights(weight_cols, weight_out, weight_down)
+        col_mats, out_mat, down_mats = full[0:7], full[7], full[8:12]
+    else:
+        col_mats = lax.all_gather(weight_cols, "tp", axis=2, tiled=True)
+        out_mat = lax.all_gather(weight_out, "tp", axis=0, tiled=True)
+        down_mats = lax.all_gather(weight_down, "tp", axis=1, tiled=True)
     x_own = hidden.astype(jnp.float32) + layout_embed(cell_boxes, cell_ids)
     x_low = x_own.astype(jnp.bfloat16)
-    col_mats, out_mat, down_mats = (weight_cols, weight_out, weight_down)
-    x_input = lax.all_gather(x_low, "tp", axis=0, tiled=True)
-    head_count = H // tp_count
-    bias_cols = lax.dynamic_slice_in_dim(vectors, tp_index * strip_width, strip_width, 0)[:, 6:]
     projected = jnp.einsum(
-        "gtd,kdc->kgtc", x_input, col_mats[0:3], preferred_element_type=jnp.float32
-    )
-    query_low = (projected[0] + bias_cols[:, 0]).astype(jnp.bfloat16)
+        "gtd,kdc->kgtc", x_low, col_mats[0:3], preferred_element_type=jnp.float32
+    )
+    query_low = (projected[0] + vectors[:, 6]).astype(jnp.bfloat16)
     key_low = projected[1].astype(jnp.bfloat16)
-    value_low = (projected[2] + bias_cols[:, 1]).astype(jnp.bfloat16)
-    context, log_total = attend(query_low, key_low, value_low, head_count)
-    attn_out = lax.psum_scatter(
-        jnp.einsum("gtc,cd->gtd", context, out_mat, preferred_element_type=jnp.float32).astype(
-            jnp.bfloat16
-        ),
-        "tp",
-        scatter_dimension=0,
-        tiled=True,
-    ).astype(jnp.float32)
+    value_low = (projected[2] + vectors[:, 7]).astype(jnp.bfloat16)
+    context, log_total = attend(query_low, key_low, value_low, H)
+    attn_out = jnp.einsum("gtc,cd->gtd", context, out_mat, preferred_element_type=jnp.float32)
     mid_out, mid_hat, mid_inv = norm_forward(
         x_own + attn_out + vectors[:, 0], vectors[:, 2], vectors[:, 3]
     )
     mid_low = mid_out.astype(jnp.bfloat16)
-    mid_input = lax.all_gather(mid_low, "tp", axis=0, tiled=True)
     up_pre = jnp.einsum(
-        "gtd,kdc->kgtc", mid_input, col_mats[3:7], preferred_element_type=jnp.float32
-    )
-    up_pre = up_pre + jnp.transpose(bias_cols[:, 2:6])[:, None, None, :]
+        "gtd,kdc->kgtc", mid_low, col_mats[3:7], preferred_element_type=jnp.float32
+    )
+    up_pre = up_pre + jnp.transpose(vectors[:, 8:12])[:, None, None, :]
     act_low = gelu_exact(up_pre).astype(jnp.bfloat16)
-    ffn_out = lax.psum_scatter(
-        jnp.einsum("kgtc,kcd->gtd", act_low, down_mats, preferred_element_type=jnp.float32).astype(
-            jnp.bfloat16
-        ),
-        "tp",
-        scatter_dimension=0,
-        tiled=True,
-    ).astype(jnp.float32)
+    ffn_out = jnp.einsum("kgtc,kcd->gtd", act_low, down_mats, preferred_element_type=jnp.float32)
     layer_out, out_hat, out_inv = norm_forward(
         mid_out + ffn_out + vectors[:, 1], vectors[:, 4], vectors[:, 5]
     )
     output_gradient = cotangent.astype(jnp.float32)
     grad_two, gain_two, shift_two = norm_backward(output_gradient, out_hat, out_inv, vectors[:, 4])
     two_low = grad_two.astype(jnp.bfloat16)
-    two_input = lax.all_gather(two_low, "tp", axis=0, tiled=True)
-    act_grad = jnp.einsum("gtd,kcd->kgtc", two_input, down_mats, preferred_element_type=jnp.float32)
+    act_grad = jnp.einsum("gtd,kcd->kgtc", two_low, down_mats, preferred_element_type=jnp.float32)
     gelu_pull = jax.vjp(gelu_exact, up_pre)[1]
     up_low = gelu_pull(act_grad)[0].astype(jnp.bfloat16)
-    mid_back = lax.psum_scatter(
-        jnp.einsum(
-            "kgtc,kdc->gtd", up_low, col_mats[3:7], preferred_element_type=jnp.float32
-        ).astype(jnp.bfloat16),
-        "tp",
-        scatter_dimension=0,
-        tiled=True,
-    ).astype(jnp.float32)
+    mid_back = jnp.einsum(
+        "kgtc,kdc->gtd", up_low, col_mats[3:7], preferred_element_type=jnp.float32
+    )
     grad_one, gain_one, shift_one = norm_backward(
         mid_back + grad_two, mid_hat, mid_inv, vectors[:, 2]
     )
     one_low = grad_one.astype(jnp.bfloat16)
-    one_input = lax.all_gather(one_low, "tp", axis=0, tiled=True)
     ctx_grad = jnp.einsum(
-        "gtd,cd->gtc", one_input, out_mat, preferred_element_type=jnp.float32
+        "gtd,cd->gtc", one_low, out_mat, preferred_element_type=jnp.float32
     ).astype(jnp.bfloat16)
     query_grad, key_grad, value_grad = attend_back(
-        query_low, key_low, value_low, log_total, ctx_grad, head_count
+        query_low, key_low, value_low, log_total, ctx_grad, H
     )
     qkv_grad = jnp.stack([query_grad, key_grad, value_grad], 0)
-    input_part = jnp.einsum(
+    input_grad = grad_one + jnp.einsum(
         "kgtc,kdc->gtd", qkv_grad, col_mats[0:3], preferred_element_type=jnp.float32
     )
-    unit_width = query_low.shape[2]
-    strip_parts = unit_width // strip_width
-
-    def split_units(array):
-        return array.reshape(array.shape[:-1] + (strip_parts, strip_width))
-
-    qkv_blocks = jnp.einsum(
-        "gtd,kgtnc->nkdc", x_input, split_units(qkv_grad), preferred_element_type=jnp.float32
-    )
-    up_blocks = jnp.einsum(
-        "gtd,kgtnc->nkdc", mid_input, split_units(up_low), preferred_element_type=jnp.float32
-    )
-    out_block = jnp.einsum(
-        "gtnc,gtd->ndc", split_units(context), one_input, preferred_element_type=jnp.float32
-    )
-    down_blocks = jnp.einsum(
-        "kgtnc,gtd->nkdc", split_units(act_low), two_input, preferred_element_type=jnp.float32
-    )
-    all_blocks = jnp.concatenate([qkv_blocks, up_blocks, out_block[:, None], down_blocks], 1)
-    shared_part = jnp.stack(
+
+    def block(text, left, right):
+        return jnp.einsum(text, left, right, preferred_element_type=jnp.float32).astype(
+            jnp.bfloat16
+        )
+
+    qkv_blocks = block("gtd,kgtc->kdc", x_low, qkv_grad)
+    up_blocks = block("gtd,kgtc->kdc", mid_low, up_low)
+    out_block = block("gtd,gtc->dc", one_low, context)[None]
+    down_blocks = block("gtd,kgtc->kdc", two_low, act_low)
+    vector_part = jnp.stack(
         [
             jnp.sum(grad_one, (0, 1)),
             jnp.sum(grad_two, (0, 1)),
@@ -237,58 +768,64 @@
             shift_one,
             gain_two,
             shift_two,
-        ],
-        1,
-    )
-    unit_part = jnp.stack(
-        [
             jnp.sum(query_grad, (0, 1), dtype=jnp.float32),
             jnp.sum(value_grad, (0, 1), dtype=jnp.float32),
         ],
-        1,
-    )
-    unit_part = jnp.concatenate(
-        [unit_part, jnp.transpose(jnp.sum(up_low, (1, 2), dtype=jnp.float32))], 1
-    )
-    placed = lax.dynamic_update_slice_in_dim(
-        jnp.zeros((MODEL_WIDTH, 6), jnp.float32), unit_part, tp_index * strip_width, 0
-    )
-    vector_part = jnp.concatenate([shared_part, placed], 1)
-    input_red = lax.psum_scatter(
-        input_part.astype(jnp.bfloat16), "tp", scatter_dimension=0, tiled=True
-    ).astype(jnp.float32)
-    block_local = all_blocks[0]
-    input_grad = input_red + grad_one
-    slot_dev = (12 + dp_count - 1) // dp_count
-    padded = jnp.concatenate(
-        [block_local, jnp.zeros((slot_dev * dp_count - 12, MODEL_WIDTH, strip_width), jnp.float32)],
         0,
     )
-    block_grad, vector_owned = (
-        lax.psum_scatter(padded.astype(jnp.bfloat16), "dp", scatter_dimension=0, tiled=True).astype(
-            jnp.float32
-        ),
-        lax.psum_scatter(
-            vector_part.astype(jnp.bfloat16), "dp", scatter_dimension=0, tiled=True
-        ).astype(jnp.float32),
-    )
-    vector_grad = lax.psum(vector_owned, "tp")
-    full_grad = lax.all_gather(block_grad.astype(jnp.bfloat16), "tp", axis=2, tiled=True).astype(
-        block_grad.dtype
+    vector_part = jnp.concatenate(
+        [vector_part, jnp.sum(up_low, (1, 2), dtype=jnp.float32)], 0
+    )
+    owned_rows = vector_moment.shape[0]
+    slot_dev = left_stat.shape[0]
+    if near_plan:
+        padded = jnp.concatenate([vector_part, jnp.zeros((4, MODEL_WIDTH), jnp.float32)], 0)
+        full_grad, vector_sum = reduce_blocks(qkv_blocks, up_blocks, out_block, down_blocks, padded)
+        vector_all = vector_sum[0:12]
+    else:
+        block_part = jnp.concatenate(
+            [
+                qkv_blocks,
+                up_blocks,
+                out_block,
+                down_blocks,
+                jnp.zeros((slot_dev * dp_count - 12, MODEL_WIDTH, MODEL_WIDTH), jnp.bfloat16),
+            ],
+            0,
+        )
+        block_owned = lax.psum_scatter(block_part, "dp", scatter_dimension=0, tiled=True)
+        full_grad = lax.psum(block_owned, "tp")
+        vector_all = lax.psum(vector_part, ("dp", "tp"))
+    vector_grad = jnp.transpose(
+        lax.dynamic_slice_in_dim(vector_all, dp_index * owned_rows, owned_rows, 1)
     )
     own_rows = lax.dynamic_slice_in_dim(full_grad, tp_index * strip_width, strip_width, 1)
+    own_cols = lax.dynamic_slice_in_dim(full_grad, tp_index * strip_width, strip_width, 2)
+    block_grad = own_cols.astype(jnp.float32)
     left_new = STAT_DECAY * left_stat + (1.0 - STAT_DECAY) * jnp.einsum(
-        "sic,sjc->sij", own_rows, full_grad, precision=PRECISE
+        "sic,sjc->sij", own_rows, full_grad, preferred_element_type=jnp.float32
     )
     right_new = STAT_DECAY * right_stat + (1.0 - STAT_DECAY) * jnp.einsum(
-        "sic,sij->scj", block_grad, full_grad, precision=PRECISE
-    )
-    precond = jnp.einsum("sij,sjc->sic", left_root, full_grad, precision=PRECISE)
-    precond = jnp.einsum("sic,scj->sij", precond, right_root, precision=PRECISE)
+        "sic,sij->scj", own_cols, full_grad, preferred_element_type=jnp.float32
+    )
+
+    def parts(array):
+        high = array.astype(jnp.bfloat16)
+        return high, (array - high.astype(jnp.float32)).astype(jnp.bfloat16)
+
+    def product(left, right):
+        return jnp.einsum("sij,sjc->sic", left, right, preferred_element_type=jnp.float32)
+
+    left_high, left_rest = parts(left_root)
+    right_high, right_rest = parts(right_root)
+    precond = product(left_high, full_grad) + product(left_rest, full_grad)
+    pre_high, pre_rest = parts(precond)
+    precond = (
+        product(pre_high, right_high) + product(pre_rest, right_high) + product(pre_high, right_rest)
+    )
     master_new = master - BLOCK_RATE * precond
     weight_copy = master_new.astype(jnp.bfloat16)
     ema_new = EMA_DECAY * averaged_weight + (1.0 - EMA_DECAY) * master_new
-    owned_rows = vector_grad.shape[0]
     vector_rows = lax.dynamic_slice_in_dim(vectors, dp_index * owned_rows, owned_rows, 0)
     moment_new = MOMENTUM * vector_moment + vector_grad
     total_tokens = page_rows * seq_len * dp_count * tp_count

time: 1050 us -> 574 us (0.55)
  waiting for transfers between devices: 774 us -> 0 us
  Pallas kernels: 0 us -> 274 us
  matrix products: 161 us -> 217 us
  other arithmetic: 57.5 us -> 38.2 us
  between operations: 14.7 us -> 1.56 us
  blocking collectives: 12.1 us -> 0 us
    all_gather x5 -> x0, waiting for transfers between devices: 388 us -> none  [the longest x1 82.2 us: local(): x_input = lax.all_gather(x_low, 'tp', axis=0, tiled=True)]
    reduce_scatter x5 -> x0, waiting for transfers between devices: 348 us -> none  [the longest x1 75.4 us: local(): lax.psum_scatter(jnp.einsum('kgtc,kdc->gtd', up_low, col_mats[3:7], prefe...]
    pallas_call x0 -> x2, Pallas kernels: none -> 274 us  [the longest x1 183 us: reduce_blocks(): pl.pallas_call(reduce_kernel, name='reduce_blocks', out_shape=(jax.ShapeD...]
    unnamed x12 -> x0, waiting for transfers between devices: 37.4 us -> none
    dot_general x12 -> x15, matrix products: 94.9 us -> 121 us  [the longest x4 45.7 us: block(): jnp.einsum(text, left, right, preferred_element_type=jnp.float32)]
    dot_general x1, matrix products: 6.05 us -> 28.4 us  [local(): jnp.einsum('kgtc,kcd->gtd', act_low, down_mats, preferred_element_type=jn...]
    psum x1 -> x0, blocking collectives: 12.1 us -> none  [local(): vector_grad = lax.psum(vector_owned, 'tp')]
    unnamed x113 -> x120, local copies, waits for them, and re-layouts: 13.1 us -> 22.5 us
  transfers between devices with their start and end apart: 11 -> 0, of which waited for: 11 -> 0; matrix products, arithmetic and copies ran while one was open for 3% -> 0% of each run, Pallas kernels for 0% -> 0%
where the time goes in v1:
time: 574 us; the launch traced here: 565 us
  Pallas kernels  274 us (48%)
  matrix products  217 us (38%)
  other arithmetic  38.2 us (7%)
  local copies, waits for them, and re-layouts  34.2 us (6%)
    pallas_call x1, Pallas kernels, reduce_blocks(): pl.pallas_call(reduce_kernel, name='reduce_blocks', out_shape=(jax.ShapeD...  183 us
    pallas_call x1, Pallas kernels, gather_weights(): pl.pallas_call(gather_kernel, name='gather_weights', out_shape=jax.ShapeD...  91.5 us
    dot_general x4, matrix products, block(): jnp.einsum(text, left, right, preferred_element_type=jnp.float32)  45.7 us
    dot_general x1, matrix products, local(): jnp.einsum('kgtc,kcd->gtd', act_low, down_mats, preferred_element_type=jn...  28.4 us
    dot_general x1, matrix products, local(): jnp.einsum('gtd,kcd->kgtc', two_low, down_mats, preferred_element_type=jn...  25.6 us
    unnamed x120, local copies, waits for them, and re-layouts  22.5 us
    dot_general x5, matrix products, product(): jnp.einsum('sij,sjc->sic', left, right, preferred_element_type=jnp.float32)  17.5 us
    convert_element_type x1, other arithmetic, attend_back(): (probs * (prob_grad - jnp.sum(probs * prob_grad, -1, keepdims=True))).ast...  11.9 us

profile of v1, /device:TPU:0, one launch (start us, length us, event | category | flops | bytes accessed | tf_op | source)
XLA Modules:
  0.0 565.5 jit_solution(15765080488485213308)
XLA Ops:
  5.3 91.5 %gather_weights.1 = bf16[12,1024,1024]{2,1,0:T(8,128)(2,1)S(1)} custom-call(bf16[7,1024,256]{2,1,0:T(8,128)(2,1)S(1)} %copy-done.1, bf16[256,1024]{1,0:T(8,128)(2,1)S(1)} %copy-done.3, bf16[4,256,1024]{2,1,0:T(8,128)(2,1)S(1)} %copy-done.2), custom_call_target="tpu_custom_call" | custom-call | tf_op jit(solution)/shard_map/gather_weights/pallas_call | solution.py:227
  96.9 8.3 %copy-done = bf16[12,1024,1024]{2,1,0:T(8,128)(2,1)} copy-done((bf16[12,1024,1024]{2,1,0:T(8,128)(2,1)}, bf16[12,1024,1024]{2,1,0:T(8,128)(2,1)S(1)}, u32[]{:S(2)}) %copy-start) | copy-done | bytes 25165848
  105.5 7.9 %multiply_sine_fusion = (f32[1,512,4,128]{3,2,1,0:T(4,128)S(1)}, f32[1,512,4,128]{3,2,1,0:T(4,128)S(1)}) fusion(f32[128]{0:T(128)S(1)} %multiply_exponential_fusion, f32[512,4]{1,0:T(8,128)S(1)} %fusion.88), kind=kLoop, calls=%fused_computation.113 | loop fusion | flops 262144 | bytes 2105856 | tf_op jit(solution)/shard_map/sin | solution.py:592
  116.1 6.4 %convolution_bitcast_fusion = f32[3,1,512,1024]{2,3,0,1:T(8,128)S(1)} fusion(bf16[12,1024,1024]{2,1,0:T(8,128)(2,1)} %copy-done, f32[1,512,1024]{2,1,0:T(8,128)} %mul.260, bf16[1,512,1024]{2,1,0:T(8,128)(2,1)S(1)} %copy-done.47), kind=kOutput, calls=%fused_computation.63 | convolution fusion | flops 3222798336 | bytes 34603008 | tf_op jit(solution)/shard_map/gtd,kdc->kgtc/dot_general | solution.py:709
  125.2 7.3 %multiply_reduce_fusion.1 = (f32[16,512]{1,0:T(8,128)S(1)}, f32[16,512,512]{1,2,0:T(8,128)}) fusion(bf16[512,16,64]{0,2,1:T(8,128)(2,1)S(1)} %bitcast.276, f32[512,16,64]{0,2,1:T(8,128)S(1)} %bitcast.272, f32[16,64]{1,0:T(8,128)S(1)} %add.153), kind=kOutput, calls=%fused_computation.4 | convolution fusion | flops 546299904 | bytes 19959808 | tf_op jit(solution)/shard_map/gqhe,gkhe->ghqk/dot_general | solution.py:620
  132.5 8.7 %exponential_reduce_fusion = f32[16,512]{1,0:T(8,128)S(1)} fusion(f32[16,512,512]{1,2,0:T(8,128)} %get-tuple-element.49, f32[16,512]{1,0:T(8,128)S(1)} %get-tuple-element.48), kind=kLoop, calls=%fused_computation.3 | loop fusion | flops 12574720 | bytes 16842752 | tf_op jit(solution)/shard_map/reduce_sum | solution.py:627
  141.4 9.0 %convolution_convert_fusion.1 = bf16[16,64,512]{2,1,0:T(8,128)(2,1)S(1)} fusion(f32[16,512,512]{1,2,0:T(8,128)} %get-tuple-element.49, f32[16,512]{1,0:T(8,128)S(1)} %log_add_fusion, f32[512,16,64]{0,2,1:T(8,128)S(1)} %bitcast.274, f32[16,64]{1,0:T(8,128)S(1)} %add.150), kind=kOutput, calls=%fused_computation.109 | convolution fusion | flops 551026688 | bytes 19959808 | tf_op jit(solution)/shard_map/ghqk,gkhe->gqhe/dot_general | solution.py:629
  154.3 11.5 %fusion.28 = f32[4,1024,512]{1,2,0:T(8,128)} fusion(bf16[12,1024,1024]{2,1,0:T(8,128)(2,1)} %copy-done, f32[1,512,1024]{2,1,0:T(8,128)S(1)} %get-tuple-element.51, f32[1024]{0:T(1024)S(1)} %bitcast.297, f32[1024]{0:T(1024)S(1)} %bitcast.287, f32[512]{0:T(512)S(1)} %add_rsqrt_fusion.1, f32[512]{0:T(512)S(1)} %broadcast_multiply_fusion.5), kind=kOutput, calls=%fused_computation.47 | convolution fusion | flops 4297588736 | bytes 18886656 | tf_op jit(solution)/shard_map/gtd,kdc->kgtc/dot_general | solution.py:721
  168.3 28.4 %fusion.118 = (f32[512]{0:T(512)S(1)}, f32[1,512,1024]{2,1,0:T(8,128)S(1)}) fusion(f32[1024]{0:T(1024)} %bitcast.302, bf16[12,1024,1024]{2,1,0:T(8,128)(2,1)S(1)} %bitcast.269, f32[4,1024,512]{1,2,0:T(8,128)} %fusion.28, f32[4,1024]{1,0:T(4,128)S(1)} %slice_bitcast_fusion, f32[1024]{0:T(1024)} %bitcast.298, f32[1024]{0:T(1024)S(1)} %bitcast.288, ...), kind=kOutput, calls=%fused_computation.175 | convolution fusion | flops 4437048832 | bytes 21006336 | tf_op jit(solution)/shard_map/kgtc,kcd->gtd/dot_general | solution.py:726
  200.3 25.6 %convert_reduce_fusion = (f32[4,1024]{1,0:T(4,128)S(1)}, bf16[4,1,512,1024]{3,2,0,1:T(8,128)(2,1)}) fusion(bf16[12,1024,1024]{2,1,0:T(8,128)(2,1)S(1)} %bitcast.269, f32[1,512,1024]{2,1,0:T(8,128)S(1)} %get-tuple-element.30, f32[4,1024]{1,0:T(4,128)S(1)} %slice_bitcast_fusion, f32[4,1024,512]{1,2,0:T(8,128)S(1)} %bitcast.307), kind=kOutput, calls=%fused_computation.26 | convolution fusion | flops 4452773888 | bytes 39878656 | tf_op jit(solution)/shard_map/gtd,kcd->kgtc/dot_general | solution.py:733
  225.9 10.4 %multiply_reduce_fusion.2 = (f32[1024]{0:T(1024)S(1)}, f32[512]{0:T(512)S(1)}, f32[512]{0:T(512)S(1)}, f32[1024]{0:T(1024)S(1)}, f32[1,512,1024]{2,1,0:T(8,128)S(1)}) fusion(f32[1,512,1024]{2,1,0:T(8,128)S(1)} %get-tuple-element.51, f32[512]{0:T(512)S(1)} %copy-done.40, f32[512]{0:T(512)S(1)} %broadcast_multiply_fusion.5, f32[1024]{0:T(1024)S(1)} %bitcast.289, ...), kind=kOutput, calls=%fused_computation.89 | convolution fusion | flops 4300207104 | bytes 18894848 | tf_op jit(solution)/shard_map/kgtc,kdc->gtd/dot_general | solution.py:736
  245.4 11.4 %multiply_reduce_fusion = (f32[16,512]{1,0:T(8,128)S(1)}, f32[16,512,512]{1,2,0:T(8,128)}) fusion(f32[16,512,512]{1,2,0:T(8,128)} %get-tuple-element.49, f32[16,512]{1,0:T(8,128)S(1)} %copy-done.33, bf16[512,16,64]{0,2,1:T(8,128)(2,1)S(1)} %bitcast.278, f32[512,16,64]{0,2,1:T(8,128)S(1)} %bitcast.275, f32[16,64]{1,0:T(8,128)S(1)} %copy-done.37), kind=kOutput, calls=%fused_computation.1 | convolution fusion | flops 554688512 | bytes 36769792 | tf_op jit(solution)/shard_map/gqhe,gkhe->ghqk/dot_general | solution.py:654
  256.8 11.9 %multiply_convert_fusion = bf16[16,512,512]{1,2,0:T(8,128)(2,1)S(1)} fusion(f32[16,512,512]{1,2,0:T(8,128)} %get-tuple-element.56, f32[16,512,512]{1,2,0:T(8,128)} %get-tuple-element.49, f32[16,512]{1,0:T(8,128)S(1)} %get-tuple-element.55, f32[16,512]{1,0:T(8,128)S(1)} %copy-done.33), kind=kLoop, calls=%fused_computation | loop fusion | flops 20971520 | bytes 42008576 | tf_op jit(solution)/shard_map/convert_element_type | solution.py:657
  274.4 8.8 %convert_reduce_fusion.2 = (f32[16,64]{1,0:T(8,128)S(1)}, bf16[16,64,512]{2,1,0:T(8,128)(2,1)}) fusion(bf16[512,16,64]{0,2,1:T(8,128)(2,1)S(1)} %bitcast.279, f32[16,512,512]{1,2,0:T(8,128)} %get-tuple-element.49, f32[16,512]{1,0:T(8,128)S(1)} %copy-done.33), kind=kOutput, calls=%fused_computation.87 | convolution fusion | flops 551025664 | bytes 18911232 | tf_op jit(solution)/shard_map/ghqk,gqhe->gkhe/dot_general | solution.py:648
  284.6 26.5 %convert_bitcast_fusion.down = bf16[4,1024,1024]{2,1,0:T(8,128)(2,1)} fusion(f32[1,512,1024]{2,1,0:T(8,128)S(1)} %copy-done.25, f32[4,1024,512]{1,2,0:T(8,128)} %fusion.28, f32[4,1024]{1,0:T(4,128)S(1)} %slice_bitcast_fusion), kind=kOutput, calls=%fused_computation.27 | convolution fusion | flops 4438097920 | bytes 18890752 | tf_op jit(solution)/shard_map/gtd,kgtc->kdc/dot_general | solution.py:755
  313.7 8.1 %convert_bitcast_fusion.1.up = bf16[4,1024,1024]{2,1,0:T(8,128)(2,1)} fusion(bf16[4,1,512,1024]{3,2,0,1:T(8,128)(2,1)S(1)} %copy-done.49, f32[1,512,1024]{2,1,0:T(8,128)S(1)} %copy-done.14, f32[1024]{0:T(1024)S(1)} %bitcast.299, f32[1024]{0:T(1024)S(1)} %bitcast.291, f32[512]{0:T(512)S(1)} %copy-done.40, f32[512]{0:T(512)S(1)} %broadcast_multiply_fusion.5), kind=kOutput, calls=%fused_computation.28 | convolution fusion | flops 4301783040 | bytes 14692352 | tf_op jit(solution)/shard_map/gtd,kgtc->kdc/dot_general | solution.py:755
  323.2 7.1 %multiply_convert_fusion.1 = bf16[16,64,512]{2,1,0:T(8,128)(2,1)} fusion(bf16[16,512,512]{1,2,0:T(8,128)(2,1)} %copy-done.4, f32[512,16,64]{0,2,1:T(8,128)S(1)} %bitcast.273, f32[16,64]{1,0:T(8,128)S(1)} %copy-done.35), kind=kOutput, calls=%fused_computation.91 | convolution fusion | flops 538968064 | bytes 11538432 | tf_op jit(solution)/shard_map/ghqk,gqhe->gkhe/dot_general | solution.py:665
  333.8 8.4 %convert_bitcast_fusion.2.qkv = bf16[3,1024,1024]{2,1,0:T(8,128)(2,1)} fusion(bf16[1,1,512,1024]{3,2,0,1:T(8,128)(2,1)S(1)} %copy.59, bf16[1,1,512,1024]{3,2,0,1:T(8,128)(2,1)S(1)} %copy.58, bf16[1,1,512,1024]{3,2,0,1:T(8,128)(2,1)} %copy.57, f32[1,512,1024]{2,1,0:T(8,128)} %mul.260, bf16[1,512,1024]{2,1,0:T(8,128)(2,1)} %param.15), kind=kOutput, calls=%fused_computation.49 | convolution fusion | flops 3229089792 | bytes 12582912 | tf_op jit(solution)/shard_map/gtd,kgtc->kdc/dot_general | solution.py:755
  342.2 182.7 %reduce_blocks.1 = (bf16[2,1024,1024]{2,1,0:T(8,128)(2,1)}, f32[16,1024]{1,0:T(8,128)}) custom-call(bf16[3,1024,1024]{2,1,0:T(8,128)(2,1)} %convert_bitcast_fusion.2.qkv, bf16[4,1024,1024]{2,1,0:T(8,128)(2,1)} %convert_bitcast_fusion.1.up, bf16[1,1024,1024]{2,1,0:T(8,128)(2,1)} %convert_bitcast_fusion.3.outb, ...), custom_call_target="tpu_custom_call" | custom-call | tf_op jit(solution)/shard_map/reduce_blocks/pallas_call | solution.py:547
  524.9 5.3 fusion.70
  532.1 4.9 fusion.71
  543.5 6.0 %add_multiply_fusion = f32[2,256,1024]{2,1,0:T(8,128)} fusion(f32[2,256,1024]{2,1,0:T(8,128)} %param.25, bf16[2,1024,1024]{2,1,0:T(8,128)(2,1)} %get-tuple-element.14, s32[]{:T(128)S(6)} %select_n.8), kind=kOutput, calls=%fused_computation.85 | convolution fusion | flops 1074790400 | bytes 9437188 | tf_op jit(solution)/shard_map/sic,sij->scj/dot_general | solution.py:808
  549.5 4.2 add_multiply_fusion.1
  557.1 8.2 %bitcast_add_fusion.2 = f32[1,512,1024]{2,1,0:T(8,128)} fusion(f32[1,512,1024]{2,1,0:T(8,128)S(1)} %copy-done.23, bf16[12,1024,1024]{2,1,0:T(8,128)(2,1)} %copy-done, bf16[1,1,512,1024]{3,2,0,1:T(8,128)(2,1)} %copy-done.31, bf16[1,1,512,1024]{3,2,0,1:T(8,128)(2,1)} %copy-done.30, bf16[1,1,512,1024]{3,2,0,1:T(8,128)(2,1)S(1)} %copy-done.29), kind=kOutput, calls=%fused_computation.71 | convolution fusion | flops 3224895488 | bytes 13631488 | tf_op jit(solution)/shard_map/kgtc,kdc->gtd/dot_general | solution.py:750
  (163 shorter events, 55.6 us)
Async XLA Ops:
  5.3 99.8 %copy-start.45 = (s32[1,512]{1,0:T(1,128)S(1)}, s32[1,512]{1,0:T(1,128)}, u32[]{:S(2)}) copy-start(s32[1,512]{1,0:T(1,128)} %param.16) | copy-start | bytes 6148
  5.3 99.8 %copy-start.46 = (s32[1,64,4]{1,2,0:T(4,128)S(1)}, s32[1,64,4]{1,2,0:T(4,128)}, u32[]{:S(2)}) copy-start(s32[1,64,4]{1,2,0:T(4,128)} %param.17) | copy-start | bytes 3076
  125.2 29.1 %copy-start.43 = (f32[1024,1]{0,1:T(1,128)}, f32[1024,1]{0,1:T(1,128)S(1)}, u32[]{:S(2)}) copy-start(f32[1024,1]{0,1:T(1,128)S(1)} %get-tuple-element.42) | copy-start | bytes 12292
  153.9 72.0 %copy-start.13 = (f32[1,512,1024]{2,1,0:T(8,128)}, f32[1,512,1024]{2,1,0:T(8,128)S(1)}, u32[]{:S(2)}) copy-start(f32[1,512,1024]{2,1,0:T(8,128)S(1)} %get-tuple-element.51) | copy-start | bytes 6291460
  153.9 11.9 %slice-start = ((s8[25165824]{0:T(1024)(128)(4,1)}), s8[4194304]{0:T(1024)(128)(4,1)S(1)}, s32[]{:S(2)}) async-start(s8[25165824]{0:T(1024)(128)(4,1)} %bitcast.268), calls=%async_computation | async-start | bytes 8388608
  154.3 11.5 %copy-start.39 = (f32[512]{0:T(512)}, f32[512]{0:T(512)S(1)}, u32[]{:S(2)}) copy-start(f32[512]{0:T(512)S(1)} %add_rsqrt_fusion.1) | copy-start | bytes 6148
  154.3 11.5 %slice-start.1 = ((s8[25165824]{0:T(1024)(128)(4,1)}), s8[4194304]{0:T(1024)(128)(4,1)S(1)}, s32[]{:S(2)}) async-start(s8[25165824]{0:T(1024)(128)(4,1)} %bitcast.268), calls=%async_computation.1 | async-start | bytes 8388608
  154.3 11.5 %slice-start.2 = ((s8[25165824]{0:T(1024)(128)(4,1)}), s8[4194304]{0:T(1024)(128)(4,1)S(1)}, s32[]{:S(2)}) async-start(s8[25165824]{0:T(1024)(128)(4,1)} %bitcast.268), calls=%async_computation.2 | async-start | bytes 8388608
  154.3 12.8 %slice-start.4 = ((s8[25165824]{0:T(1024)(128)(4,1)}), s8[4194304]{0:T(1024)(128)(4,1)S(1)}, s32[]{:S(2)}) async-start(s8[25165824]{0:T(1024)(128)(4,1)} %bitcast.268), calls=%async_computation.4 | async-start | bytes 8388608
  154.3 14.0 %slice-start.5 = ((s8[25165824]{0:T(1024)(128)(4,1)}), s8[4194304]{0:T(1024)(128)(4,1)S(1)}, s32[]{:S(2)}) async-start(s8[25165824]{0:T(1024)(128)(4,1)} %bitcast.268), calls=%async_computation.5 | async-start | bytes 8388608
  165.8 34.5 %slice-start.8 = ((s8[8388608]{0:T(1024)(128)(4,1)}), s8[4194304]{0:T(1024)(128)(4,1)S(1)}, s32[]{:S(2)}) async-start(s8[8388608]{0:T(1024)(128)(4,1)} %bitcast.306), calls=%async_computation.8 | async-start | bytes 8388608
  168.3 28.8 %copy-start.17 = (bf16[1,512,1024]{2,1,0:T(8,128)(2,1)S(1)}, bf16[1,512,1024]{2,1,0:T(8,128)(2,1)}, u32[]{:S(2)}) copy-start(bf16[1,512,1024]{2,1,0:T(8,128)(2,1)} %param.18) | copy-start | bytes 3145732
  168.3 32.0 %slice-start.9 = ((s8[8388608]{0:T(1024)(128)(4,1)}), s8[4194304]{0:T(1024)(128)(4,1)S(1)}, s32[]{:S(2)}) async-start(s8[8388608]{0:T(1024)(128)(4,1)} %bitcast.306), calls=%async_computation.9 | async-start | bytes 8388608
  200.2 25.6 %copy-start.24 = (f32[1,512,1024]{2,1,0:T(8,128)}, f32[1,512,1024]{2,1,0:T(8,128)S(1)}, u32[]{:S(2)}) copy-start(f32[1,512,1024]{2,1,0:T(8,128)S(1)} %get-tuple-element.30) | copy-start | bytes 6291460
  200.2 25.6 %copy-start.40 = (f32[512]{0:T(512)S(1)}, f32[512]{0:T(512)}, u32[]{:S(2)}) copy-start(f32[512]{0:T(512)} %copy-done.39) | copy-start | bytes 6148
  256.8 15.1 %copy-start.12 = (bf16[1,1,512,1024]{2,3,0,1:T(8,128)(2,1)S(1)}, bf16[1,1,512,1024]{2,3,0,1:T(8,128)(2,1)}, u32[]{:S(2)}) copy-start(bf16[1,1,512,1024]{2,3,0,1:T(8,128)(2,1)} %copy-done.11) | copy-start | bytes 3145732
  284.5 26.5 %copy-start.22 = (f32[1,512,1024]{2,1,0:T(8,128)S(1)}, f32[1,512,1024]{2,1,0:T(8,128)}, u32[]{:S(2)}) copy-start(f32[1,512,1024]{2,1,0:T(8,128)} %copy-done.21) | copy-start | bytes 6291460
  284.5 26.5 %copy-start.28 = (bf16[16,64,512]{2,1,0:T(8,128)(2,1)S(1)}, bf16[16,64,512]{2,1,0:T(8,128)(2,1)}, u32[]{:S(2)}) copy-start(bf16[16,64,512]{2,1,0:T(8,128)(2,1)} %copy-done.27) | copy-start | bytes 3145732
  284.5 29.2 %copy-start.14 = (f32[1,512,1024]{2,1,0:T(8,128)S(1)}, f32[1,512,1024]{2,1,0:T(8,128)}, u32[]{:S(2)}) copy-start(f32[1,512,1024]{2,1,0:T(8,128)} %copy-done.13) | copy-start | bytes 6291460
  284.5 29.2 %copy-start.44 = (f32[1024,1]{0,1:T(1,128)S(1)}, f32[1024,1]{0,1:T(1,128)}, u32[]{:S(2)}) copy-start(f32[1024,1]{0,1:T(1,128)} %copy-done.43) | copy-start | bytes 12292
  284.5 29.2 %copy-start.49 = (bf16[4,1,512,1024]{3,2,0,1:T(8,128)(2,1)S(1)}, bf16[4,1,512,1024]{3,2,0,1:T(8,128)(2,1)}, u32[]{:S(2)}) copy-start(bf16[4,1,512,1024]{3,2,0,1:T(8,128)(2,1)} %get-tuple-element.62) | copy-start | bytes 12582916
  543.5 11.8 %copy-start.41 = (f32[128,12]{0,1:T(8,128)S(1)}, f32[128,12]{0,1:T(8,128)}, u32[]{:S(2)}) copy-start(f32[128,12]{0,1:T(8,128)} %param.23) | copy-start | bytes 18436
  543.5 13.6 %copy-start.23 = (f32[1,512,1024]{2,1,0:T(8,128)S(1)}, f32[1,512,1024]{2,1,0:T(8,128)}, u32[]{:S(2)}) copy-start(f32[1,512,1024]{2,1,0:T(8,128)} %copy-done.21) | copy-start | bytes 6291460
  543.5 13.6 %copy-start.29 = (bf16[1,1,512,1024]{3,2,0,1:T(8,128)(2,1)S(1)}, bf16[1,1,512,1024]{3,2,0,1:T(8,128)(2,1)}, u32[]{:S(2)}) copy-start(bf16[1,1,512,1024]{3,2,0,1:T(8,128)(2,1)} %copy.57) | copy-start | bytes 3145732
  (36 other events, 230.6 us)
